TPU v7x, 256 devices: a whole 4x4x8 slice. The times are simulated.
256 devices in a mesh: blk: 32 (over x, z_lo, core), uly: 8 (over y, z_hi).
Axes of the slice: x: 4, y: 4, z: 8 (z_hi: 2, z_lo: 4; z = z_hi * 4 + z_lo), core: 2. Of those that a mesh axis runs over, the one named last changes fastest.
Arguments:
- video_tokens: bfloat16 [12288, 3072], P(('blk', 'uly')), may hold values from -6 to 6
- text_tokens: bfloat16 [256, 3072], P('uly'), may hold values from -6 to 6
- video_modulation: bfloat16 [3, 3072], replicated, may hold values from -4 to 4
- text_modulation: bfloat16 [3, 3072], replicated, may hold values from -4 to 4
- video_projection: bfloat16 [3072, 3, 2048], P(None, None, 'uly'), may hold values from -0.109375 to 0.109375
- text_projection: bfloat16 [3072, 3, 2048], P(None, None, 'uly'), may hold values from -0.109375 to 0.109375
- video_output: bfloat16 [2048, 3072], P('uly'), may hold values from -0.125 to 0.125
- text_output: bfloat16 [2048, 3072], P('uly'), may hold values from -0.125 to 0.125
- video_gains: float32 [2, 128], replicated, may hold values from 1 to 12
- text_gains: float32 [2, 128], replicated, may hold values from 1 to 12
Outputs:
- video_attention: bfloat16 [12288, 3072], P(('blk', 'uly'))
- text_attention: bfloat16 [256, 3072], P('uly')
All inputs are finite; a program needn't handle non-finite values.
Results may differ from a plain program's by a relative error of at most 0.025.
The roundings to bfloat16 on the way count: a program that leaves them out, or rounds other values in their place, can miss the bound.
Values may be sent and summed in bfloat16 or wider, within the bound.
A program may use at most 128 MiB of HBM per device.

v0:
```python
import jax
import jax.numpy as jnp
from jax import lax
from jax.sharding import Mesh
from jax.sharding import PartitionSpec as P

HD = 128
BLK = ("blk_0", "blk_1", "blk_2")
ULY = ("uly_0", "uly_1")
BLK_ULY = ("blk_0", "blk_1", "blk_2", "uly_0", "uly_1")
EPS_NORM = 1e-06


def collected_together(x, axis):
    leaves = jax.tree.leaves(x)
    turns = sorted(range(len(leaves)), key=lambda k: -leaves[k].size)
    width = (1, *leaves[turns[0]].shape)[-1]
    lines = [
        jnp.pad(leaves[k].reshape(-1), (0, -leaves[k].size % width)).reshape(-1, width)
        for k in turns
    ]
    both, at, found = (lax.all_gather(jnp.concatenate(lines), axis), 0, {})
    for k, line in zip(turns, lines):
        slab = both[:, at : at + len(line)].reshape(len(both), -1)
        found[k] = slab[:, : leaves[k].size].reshape(-1, *leaves[k].shape)
        at += len(line)
    numbers = iter(range(len(leaves)))
    return jax.tree.map(lambda _: found[next(numbers)], x)


def merged_by_axis(x, axes, combine):
    for axis in axes:
        pieces = collected_together(
            jax.tree.map(
                lambda part, kind: part.astype(kind),
                x,
                jax.tree.map(lambda a: jnp.bfloat16 if a.dtype == jnp.float32 else a.dtype, x),
            ),
            axis,
        )
        widened = [
            jax.tree.map(lambda part, own: part[k].astype(own.dtype), pieces, x)
            for k in range(lax.axis_size(axis))
        ]
        x = widened[0]
        for partner_block in widened[1:]:
            x = combine(x, partner_block)
    return x


def summed_rows(terms, axes):
    subtotal = terms.astype(jnp.bfloat16)
    for axis in axes:
        subtotal = lax.psum_scatter(subtotal, axis, scatter_dimension=0, tiled=True)
    return subtotal.astype(jnp.float32)


def split_up(x, dim, length):
    before, after = (x.shape[:dim], x.shape[dim + 1 :])
    return jnp.moveaxis(x.reshape(*before, length, -1, *after), dim, 0)


def summed_on_arrival(x, axis, dim):
    length = lax.axis_size(axis)
    tiles = lax.all_to_all(split_up(x, dim, length), axis, 0, 0, tiled=True)
    return jnp.sum(tiles.astype(jnp.float32), axis=0)


def modulate(rows, factors):
    floats = rows.astype(jnp.float32)
    centre = floats - jnp.mean(floats, axis=-1, keepdims=True)
    spread = jnp.mean(centre * centre, axis=-1, keepdims=True)
    normed = centre / jnp.sqrt(spread + EPS_NORM)
    wide = factors.astype(jnp.float32)
    return (normed * (1.0 + wide[1]) + wide[0]).astype(jnp.bfloat16)


def head_norm(vectors, channel_gain):
    inverse = lax.rsqrt(jnp.mean(vectors * vectors, axis=-1, keepdims=True) + EPS_NORM)
    return (vectors * inverse * channel_gain).astype(jnp.bfloat16)


def project_rows(modded, weights, gains):
    mixture = jnp.einsum("td,dch->tch", modded, weights, preferred_element_type=jnp.float32)
    row_count, col_count = (mixture.shape[0], mixture.shape[2])
    per_head = mixture.reshape(row_count, 3, col_count // HD, HD)
    query_rows = head_norm(per_head[:, 0], gains[0]).reshape(row_count, col_count)
    key_rows = head_norm(per_head[:, 1], gains[1]).reshape(row_count, col_count)
    value_rows = per_head[:, 2].astype(jnp.bfloat16).reshape(row_count, col_count)
    return jnp.stack([query_rows, key_rows, value_rows], axis=1)


def block_scores(query_rows, key_rows):
    heads_here = query_rows.shape[1] // HD
    return jnp.einsum(
        "qhd,khd->hqk",
        query_rows.reshape(-1, heads_here, HD),
        key_rows.reshape(-1, heads_here, HD),
        preferred_element_type=jnp.float32,
    ) * HD ** (-0.5)


def weighted(weights, value_rows):
    heads_here = weights.shape[0]
    return jnp.einsum(
        "hqk,khd->hqd",
        weights.astype(jnp.bfloat16),
        value_rows.reshape(-1, heads_here, HD),
        preferred_element_type=jnp.float32,
    )


def opening(query_rows, key_rows, value_rows):
    scores = block_scores(query_rows, key_rows)
    highest = jnp.max(scores, axis=-1)
    weights = jnp.exp(scores - highest[..., None])
    return (highest, jnp.sum(weights, axis=-1), weighted(weights, value_rows))


def absorb(softmax_state, query_rows, key_rows, value_rows):
    highest, totals, weighted_sums = softmax_state
    scores = block_scores(query_rows, key_rows)
    raised = jnp.maximum(highest, jnp.max(scores, axis=-1))
    shrink = jnp.exp(highest - raised)
    weights = jnp.exp(scores - raised[..., None])
    return (
        raised,
        totals * shrink + jnp.sum(weights, axis=-1),
        weighted_sums * shrink[..., None] + weighted(weights, value_rows),
    )


def combine_states(earlier_state, later_state):
    raised = jnp.maximum(earlier_state[0], later_state[0])
    left_scale = jnp.exp(earlier_state[0] - raised)
    right_scale = jnp.exp(later_state[0] - raised)
    totals = earlier_state[1] * left_scale + later_state[1] * right_scale
    weighted_sums = (
        earlier_state[2] * left_scale[..., None] + later_state[2] * right_scale[..., None]
    )
    return (raised, totals, weighted_sums)


def finalize(softmax_state):
    result = softmax_state[2] / softmax_state[1][..., None]
    return jnp.transpose(result, (1, 0, 2)).reshape(result.shape[1], -1).astype(jnp.bfloat16)


def joint_attention(softmax_state, query_rows, pairs):
    shard_rows = pairs.shape[0]
    piece_rows = lax.all_gather(pairs, BLK, axis=0, tiled=True)
    turn_count = piece_rows.shape[0] // shard_rows
    turn_rows = piece_rows.shape[0] // turn_count

    def one_turn(turn_index, inner_state):
        sliced = lax.dynamic_slice_in_dim(piece_rows, turn_index * turn_rows, turn_rows, 0)
        return absorb(inner_state, query_rows, sliced[:, 0], sliced[:, 1])

    return lax.fori_loop(0, turn_count, one_turn, softmax_state)


def local(
    video_tokens,
    text_tokens,
    video_modulation,
    text_modulation,
    video_projection,
    text_projection,
    video_output,
    text_output,
    video_gains,
    text_gains,
):
    video_proj = project_rows(
        lax.all_gather(modulate(video_tokens, video_modulation), ULY, axis=0, tiled=True),
        video_projection,
        video_gains,
    )
    text_proj = project_rows(
        lax.all_gather(modulate(text_tokens, text_modulation), ULY, axis=0, tiled=True),
        text_projection,
        text_gains,
    )
    video_pairs = video_proj[:, 1:]
    video_state = opening(video_proj[:, 0], text_proj[:, 1], text_proj[:, 2])
    video_heads = finalize(joint_attention(video_state, video_proj[:, 0], video_pairs))
    text_state = opening(text_proj[:, 0], video_proj[:, 1], video_proj[:, 2])
    text_state = merged_by_axis(text_state, BLK, combine_states)
    text_heads = finalize(absorb(text_state, text_proj[:, 0], text_proj[:, 1], text_proj[:, 2]))
    video_summed = summed_rows(
        jnp.dot(video_heads, video_output, preferred_element_type=jnp.float32), ULY
    )
    text_summed = summed_on_arrival(
        jnp.dot(text_heads, text_output, preferred_element_type=jnp.float32).astype(jnp.bfloat16),
        ULY,
        0,
    )
    video_attention = (video_summed * video_modulation[2].astype(jnp.float32)).astype(jnp.bfloat16)
    text_attention = (text_summed * text_modulation[2].astype(jnp.float32)).astype(jnp.bfloat16)
    return (video_attention, text_attention)


def solution(mesh):
    torus = Mesh(mesh.devices.reshape(4, 4, 2, 4, 2), ("blk_0", "blk_1", "blk_2", "uly_0", "uly_1"))
    placed = (
        P(BLK_ULY, None),
        P(ULY, None),
        P(),
        P(),
        P(None, None, ULY),
        P(None, None, ULY),
        P(ULY, None),
        P(ULY, None),
        P(),
        P(),
    )
    return jax.shard_map(
        local,
        mesh=torus,
        in_specs=placed,
        out_specs=(P(BLK_ULY, None), P(ULY, None)),
        check_vma=False,
    )
```

profile of v0, /device:TPU:32, one launch (start us, length us, event | category | flops | bytes accessed | tf_op | source)
XLA Modules:
  0.0 410.6 jit_solution(2178064178969076653)
XLA Ops:
  8.9 1.1 convert_reduce_fusion.1
  10.0 1.2 fusion.17
  11.2 1.9 fusion.20
  14.6 80.3 %all-gather.7.cloned.1.call-done = bf16[384,3072]{1,0:T(8,128)(2,1)} async-done(((bf16[48,3072]{1,0:T(8,128)(2,1)}), bf16[384,3072]{1,0:T(8,128)(2,1)}) %all-gather.7.cloned.1.call-update) | async-done | bytes 2359312 | tf_op jit(solution)/shard_map/all_gather | solution.py:175
  94.9 5.3 %fusion.5 = f32[384,3,256]{0,2,1:T(8,128)S(1)} fusion(bf16[3072,3,256]{2,0,1:T(8,128)(2,1)} %param.16, bf16[384,3072]{1,0:T(8,128)(2,1)} %all-gather.7.cloned.1.call-done), kind=kOutput, calls=%fused_computation.14 | convolution fusion | flops 1811939328 | bytes 8257536 | tf_op jit(solution)/shard_map/td,dch->tch/dot_general | solution.py:84
  103.9 59.1 %all-gather.9.cloned.1.call-done = bf16[256,3072]{1,0:T(8,128)(2,1)} async-done(((bf16[32,3072]{1,0:T(8,128)(2,1)}), bf16[256,3072]{1,0:T(8,128)(2,1)}) %all-gather.9.cloned.1.call-update) | async-done | bytes 1572880 | tf_op jit(solution)/shard_map/all_gather | solution.py:180
  162.9 5.6 %fusion.7 = f32[256,3,256]{0,2,1:T(8,128)} fusion(bf16[3072,3,256]{2,0,1:T(8,128)(2,1)} %param.17, bf16[256,3072]{1,0:T(8,128)(2,1)} %all-gather.9.cloned.1.call-done), kind=kOutput, calls=%fused_computation.16 | convolution fusion | flops 1207959552 | bytes 7077888 | tf_op jit(solution)/shard_map/td,dch->tch/dot_general | solution.py:84
  171.9 1.2 fusion.156
  175.3 14.7 %all-gather = bf16[2080,128]{1,0:T(8,128)(2,1)S(1)} all-gather(bf16[520,128]{1,0:T(8,128)(2,1)S(1)} %pad_maximum_fusion.1), channel_id=2, replica_groups=mesh['blk_0'=4,'blk_1'=4,'blk_2'=2,'uly_0'=4,'uly_1'=2] {'blk_0'}, dimensions={0}, use_global_device_ids=true | all-gather | bytes 665600 | tf_op jit(solution)/shard_map/all_gather | solution.py:22
  191.7 52.5 %all-gather.11.cloned.1.call-done = bf16[12288,2,256]{0,2,1:T(8,128)(2,1)} async-done(((bf16[384,2,256]{0,2,1:T(8,128)(2,1)}), bf16[12288,2,256]{0,2,1:T(8,128)(2,1)}) %all-gather.11.cloned.1.call-update) | async-done | bytes 12582928 | tf_op jit(solution)/shard_map/all_gather | solution.py:151
  244.2 71.0 %while.17 = (s32[]{:T(128)}, f32[2,384]{1,0:T(2,128)S(1)}, f32[2,384]{1,0:T(2,128)S(1)}, f32[2,384,128]{2,1,0:T(8,128)S(1)}, bf16[12288,2,256]{0,2,1:T(8,128)(2,...) while((s32[]{:T(128)}, f32[2,384]{1,0:T(2,128)S(1)}, ...), condition=%wide.region_12.13_spmd, body=%wide.region_9.12_spmd.sunk | while | flops 152962560 | bytes 5750959 | solution.py:159
  246.4 1.1 constant_dynamic-slice_fusion.3
  248.7 1.1 constant_dynamic-slice_fusion.3
  250.9 1.1 constant_dynamic-slice_fusion.3
  253.1 1.1 constant_dynamic-slice_fusion.3
  255.3 1.1 constant_dynamic-slice_fusion.3
  257.5 1.1 constant_dynamic-slice_fusion.3
  259.8 1.1 constant_dynamic-slice_fusion.3
  262.0 1.1 constant_dynamic-slice_fusion.3
  264.2 1.1 constant_dynamic-slice_fusion.3
  266.4 1.1 constant_dynamic-slice_fusion.3
  268.6 1.1 constant_dynamic-slice_fusion.3
  270.9 1.1 constant_dynamic-slice_fusion.3
  273.1 1.1 constant_dynamic-slice_fusion.3
  275.3 1.1 constant_dynamic-slice_fusion.3
  277.5 1.1 constant_dynamic-slice_fusion.3
  279.7 1.1 constant_dynamic-slice_fusion.3
  282.0 1.1 constant_dynamic-slice_fusion.3
  284.2 1.1 constant_dynamic-slice_fusion.3
  286.4 1.1 constant_dynamic-slice_fusion.3
  288.6 1.1 constant_dynamic-slice_fusion.3
  290.8 1.1 constant_dynamic-slice_fusion.3
  293.1 1.1 constant_dynamic-slice_fusion.3
  295.3 1.1 constant_dynamic-slice_fusion.3
  297.5 1.1 constant_dynamic-slice_fusion.3
  299.7 1.1 constant_dynamic-slice_fusion.3
  301.9 1.1 constant_dynamic-slice_fusion.3
  304.2 1.1 constant_dynamic-slice_fusion.3
  306.4 1.1 constant_dynamic-slice_fusion.3
  308.6 1.1 constant_dynamic-slice_fusion.3
  315.5 2.2 convolution_convert_fusion
  317.7 15.7 %all-gather.1 = bf16[2080,128]{1,0:T(8,128)(2,1)S(1)} all-gather(bf16[520,128]{1,0:T(8,128)(2,1)S(1)} %pad_maximum_fusion.2), channel_id=3, replica_groups=mesh['blk_0'=4,'blk_1'=4,'blk_2'=2,'uly_0'=4,'uly_1'=2] {'blk_1'}, dimensions={0}, use_global_device_ids=true | all-gather | bytes 665600 | tf_op jit(solution)/shard_map/all_gather | solution.py:22
  334.0 2.0 all-gather.2
  337.8 1.8 convolution_convert_fusion.1
  339.5 6.8 %all-to-all-start = ((bf16[8,32,3072]{2,1,0:T(8,128)(2,1)}), bf16[8,32,3072]{2,1,0:T(8,128)(2,1)S(1)}, u32[]{:S(2)}, u32[]{:S(2)}) async-start(bf16[8,32,3072]{2,1,0:T(8,128)(2,1)} %bitcast.68), calls=%async_computation.2 | async-start | bytes 3145728 | tf_op jit(solution)/shard_map/all_to_all | solution.py:65
  346.4 4.9 %reduce-scatter.3.cloned.1.call-done = bf16[96,3072]{1,0:T(8,128)(2,1)} async-done(((bf16[384,3072]{1,0:T(8,128)(2,1)}), bf16[96,3072]{1,0:T(8,128)(2,1)}) %reduce-scatter.3.cloned.1.call-update) | async-done | bytes 589840 | tf_op jit(solution)/shard_map/reduce_scatter | solution.py:54
  351.4 50.1 %all-to-all-done = bf16[8,32,3072]{2,1,0:T(8,128)(2,1)S(1)} async-done(((bf16[8,32,3072]{2,1,0:T(8,128)(2,1)}), bf16[8,32,3072]{2,1,0:T(8,128)(2,1)S(1)}, u32[]{:S(2)}, u32[]{:S(2)}) %all-to-all-start) | async-done | bytes 1572896 | tf_op jit(solution)/shard_map/all_to_all | solution.py:65
  402.4 1.7 multiply_convert_fusion
  (303 shorter events, 55.6 us)
Async XLA Ops:
  7.2 308.3 %copy-start = (bf16[256,3072]{1,0:T(8,128)(2,1)S(1)}, bf16[256,3072]{1,0:T(8,128)(2,1)}, u32[]{:S(2)}) copy-start(bf16[256,3072]{1,0:T(8,128)(2,1)} %param.18) | copy-start | bytes 4718596
  7.2 6.0 %copy-start.9 = (bf16[3,3072]{1,0:T(4,128)(2,1)S(1)}, bf16[3,3072]{1,0:T(4,128)(2,1)}, u32[]{:S(2)}) copy-start(bf16[3,3072]{1,0:T(4,128)(2,1)} %param.15) | copy-start | bytes 55300
  7.2 6.0 %copy-start.3 = (bf16[32,3072]{1,0:T(8,128)(2,1)S(1)}, bf16[32,3072]{1,0:T(8,128)(2,1)}, u32[]{:S(2)}) copy-start(bf16[32,3072]{1,0:T(8,128)(2,1)} %param.13) | copy-start | bytes 589828
  7.2 7.4 %copy-start.10 = (f32[2,128]{1,0:T(2,128)S(1)}, f32[2,128]{1,0:T(2,128)}, u32[]{:S(2)}) copy-start(f32[2,128]{1,0:T(2,128)} %param.21) | copy-start | bytes 3076
  7.2 7.4 %copy-start.11 = (f32[2,128]{1,0:T(2,128)S(1)}, f32[2,128]{1,0:T(2,128)}, u32[]{:S(2)}) copy-start(f32[2,128]{1,0:T(2,128)} %param.20) | copy-start | bytes 3076
  7.2 87.7 %all-gather.7.cloned.1.call-start = ((), (), s32[]{:S(2)}) async-start(), calls=%async_computation.3 | async-start | bytes 2654208 | tf_op jit(solution)/shard_map/all_gather | solution.py:175
  13.1 149.8 %all-gather.9.cloned.1.call-start = ((), (), s32[]{:S(2)}) async-start(), calls=%async_computation.4 | async-start | bytes 1769472 | tf_op jit(solution)/shard_map/all_gather | solution.py:180
  14.5 229.7 %all-gather.11.cloned.1.call-start = ((), (), s32[]{:S(2)}) async-start(), calls=%async_computation.5 | async-start | bytes 12976128 | tf_op jit(solution)/shard_map/all_gather | solution.py:151
  102.1 0.9 copy-start.6
  103.8 247.5 %reduce-scatter.3.cloned.1.call-start = ((), (), s32[]{:S(2)}) async-start(), calls=%async_computation.6 | async-start | bytes 2949120 | tf_op jit(solution)/shard_map/reduce_scatter | solution.py:54
  171.3 1.8 copy-start.5
  174.9 15.6 %copy-start.1 = (f32[384,1,2,128]{3,0,2,1:T(8,128)S(1)}, f32[384,1,2,128]{3,0,2,1:T(8,128)}, u32[]{:S(2)}) copy-start(f32[384,1,2,128]{3,0,2,1:T(8,128)} %copy.54) | copy-start | bytes 1179652
  190.5 0.9 copy-start.7
  317.7 18.6 %copy-start.2 = (f32[2,256,256]{1,2,0:T(8,128)S(1)}, f32[2,256,256]{1,2,0:T(8,128)}, u32[]{:S(2)}) copy-start(f32[2,256,256]{1,2,0:T(8,128)} %get-tuple-element.171) | copy-start | bytes 1572868
  336.3 1.4 copy-start.4
  339.5 6.9 %copy-start.8 = (bf16[3,3072]{1,0:T(4,128)(2,1)S(1)}, bf16[3,3072]{1,0:T(4,128)(2,1)}, u32[]{:S(2)}) copy-start(bf16[3,3072]{1,0:T(4,128)(2,1)} %param.14) | copy-start | bytes 55300
  339.5 61.9 %all-to-all-start = ((bf16[8,32,3072]{2,1,0:T(8,128)(2,1)}), bf16[8,32,3072]{2,1,0:T(8,128)(2,1)S(1)}, u32[]{:S(2)}, u32[]{:S(2)}) async-start(bf16[8,32,3072]{2,1,0:T(8,128)(2,1)} %bitcast.68), calls=%async_computation.2 | async-start | bytes 3145728 | tf_op jit(solution)/shard_map/all_to_all | solution.py:65
  346.3 56.1 %reduce-scatter.5.cloned.1.call-start = ((), (), s32[]{:S(2)}) async-start(), calls=%async_computation.7 | async-start | bytes 884736 | tf_op jit(solution)/shard_map/reduce_scatter | solution.py:54
Sparse Core Ops, SparseCore 0:
  13.2 81.6 all-gather.6
  98.1 64.7 all-gather.8
  164.7 79.4 all-gather.10
  317.8 33.4 reduce-scatter.2
  353.7 44.8 reduce-scatter.4
where the time goes:
time: 412 us; the launch traced here: 411 us
  waiting for transfers between devices  247 us (60%)
  matrix products  46.4 us (11%)
  local copies, waits for them, and re-layouts  43.2 us (10%)
  blocking collectives  32.4 us (8%)
  other arithmetic  18.7 us (5%)
  between operations  14.3 us (3%)
  starting transfers between devices  7 us (2%)
    all_gather x1, waiting for transfers between devices, local(): lax.all_gather(modulate(video_tokens, video_modulation), ULY, axis=0, til...  80.3 us
    all_gather x1, waiting for transfers between devices, local(): lax.all_gather(modulate(text_tokens, text_modulation), ULY, axis=0, tiled...  59.1 us
    all_gather x1, waiting for transfers between devices, joint_attention(): piece_rows = lax.all_gather(pairs, BLK, axis=0, tiled=True)  52.5 us
    all_to_all x1, waiting for transfers between devices, summed_on_arrival(): tiles = lax.all_to_all(split_up(x, dim, length), axis, 0, 0, tiled=True)  50.1 us
    slice x32, local copies, waits for them, and re-layouts, one_turn(): return absorb(inner_state, query_rows, sliced[:, 0], sliced[:, 1])  34.2 us
    all_gather x3, blocking collectives, collected_together(): both, at, found = (lax.all_gather(jnp.concatenate(lines), axis), 0, {})  32.4 us
    dot_general x35, matrix products, weighted(): jnp.einsum('hqk,khd->hqd', weights.astype(jnp.bfloat16), value_rows.resha...  17.2 us
    dot_general x35, matrix products, block_scores(): jnp.einsum('qhd,khd->hqk', query_rows.reshape(-1, heads_here, HD), key_ro...  14.2 us
  transfers between devices with their start and end apart: 6, of which 5 were waited for; matrix products, arithmetic and copies ran while one was open for 7% of the time, Pallas kernels for 0%

commit v1 on v0

--- a/solution.py
+++ b/solution.py
@@ -148,7 +148,9 @@
 
 def joint_attention(softmax_state, query_rows, pairs):
     shard_rows = pairs.shape[0]
-    piece_rows = lax.all_gather(pairs, BLK, axis=0, tiled=True)
+    piece_rows = jnp.concatenate(
+        lax.all_to_all(jnp.stack([pairs] * lax.axis_size(BLK)), BLK, 0, 0), axis=0
+    )
     turn_count = piece_rows.shape[0] // shard_rows
     turn_rows = piece_rows.shape[0] // turn_count
 

time: 412 us -> 633 us (1.54)
  waiting for transfers between devices: 247 us -> 389 us
  matrix products: 46.4 us -> 76.7 us
  local copies, waits for them, and re-layouts: 43.2 us -> 73.2 us
  blocking collectives: 32.4 us -> 42.2 us
    all_to_all x0 -> x1, waiting for transfers between devices: none -> 161 us  [joint_attention(): lax.all_to_all(jnp.stack([pairs] * lax.axis_size(BLK)), BLK, 0, 0)]
    all_gather x1 -> x0, waiting for transfers between devices: 52.5 us -> none  [joint_attention(): piece_rows = lax.all_gather(pairs, BLK, axis=0, tiled=True)]
    all_gather x1, waiting for transfers between devices: 59.1 us -> 92.3 us  [local(): lax.all_gather(modulate(text_tokens, text_modulation), ULY, axis=0, tiled...]
    dot_general x35, matrix products: 14.2 us -> 45.4 us  [block_scores(): jnp.einsum('qhd,khd->hqk', query_rows.reshape(-1, heads_here, HD), key_ro...]
    all_to_all x0 -> x1, local copies, waits for them, and re-layouts: none -> 16.6 us  [joint_attention(): lax.all_to_all(jnp.stack([pairs] * lax.axis_size(BLK)), BLK, 0, 0)]
    while x32 -> x96, local copies, waits for them, and re-layouts: 0.08 us -> 10.4 us
    all_gather x3, blocking collectives: 32.4 us -> 42.2 us  [collected_together(): both, at, found = (lax.all_gather(jnp.concatenate(lines), axis), 0, {})]
    another operation x0 -> x1, local copies, waits for them, and re-layouts: none -> 6.6 us  [joint_attention(): jnp.stack([pairs] * lax.axis_size(BLK))]
  transfers between devices with their start and end apart: 6 -> 6, of which waited for: 5 -> 5; matrix products, arithmetic and copies ran while one was open for 7% -> 3% of each run, Pallas kernels for 0% -> 0%
where the time goes in v1:
time: 633 us; the launch traced here: 628 us
  waiting for transfers between devices  389 us (61%)
  matrix products  76.7 us (12%)
  local copies, waits for them, and re-layouts  73.2 us (12%)
  blocking collectives  42.2 us (7%)
  other arithmetic  19.3 us (3%)
  between operations  14.3 us (2%)
  starting transfers between devices  11.4 us (2%)
    all_to_all x1, waiting for transfers between devices, joint_attention(): lax.all_to_all(jnp.stack([pairs] * lax.axis_size(BLK)), BLK, 0, 0)  161 us
    all_gather x1, waiting for transfers between devices, local(): lax.all_gather(modulate(text_tokens, text_modulation), ULY, axis=0, tiled...  92.3 us
    all_gather x1, waiting for transfers between devices, local(): lax.all_gather(modulate(video_tokens, video_modulation), ULY, axis=0, til...  81.8 us
    all_to_all x1, waiting for transfers between devices, summed_on_arrival(): tiles = lax.all_to_all(split_up(x, dim, length), axis, 0, 0, tiled=True)  48 us
    dot_general x35, matrix products, block_scores(): jnp.einsum('qhd,khd->hqk', query_rows.reshape(-1, heads_here, HD), key_ro...  45.4 us
    all_gather x3, blocking collectives, collected_together(): both, at, found = (lax.all_gather(jnp.concatenate(lines), axis), 0, {})  42.2 us
    slice x32, local copies, waits for them, and re-layouts, one_turn(): return absorb(inner_state, query_rows, sliced[:, 0], sliced[:, 1])  33.7 us
    dot_general x35, matrix products, weighted(): jnp.einsum('hqk,khd->hqd', weights.astype(jnp.bfloat16), value_rows.resha...  17.3 us
  transfers between devices with their start and end apart: 6, of which 5 were waited for; matrix products, arithmetic and copies ran while one was open for 3% of the time, Pallas kernels for 0%

profile of v1, /device:TPU:32, one launch (start us, length us, event | category | flops | bytes accessed | tf_op | source)
XLA Modules:
  0.0 628.3 jit_solution(13744087210492524389)
XLA Ops:
  11.2 1.9 fusion.20
  13.1 81.8 %all-gather.6.cloned.1.call-done = bf16[384,3072]{1,0:T(8,128)(2,1)} async-done(((bf16[48,3072]{1,0:T(8,128)(2,1)}), bf16[384,3072]{1,0:T(8,128)(2,1)}) %all-gather.6.cloned.1.call-update) | async-done | bytes 2359312 | tf_op jit(solution)/shard_map/all_gather | solution.py:177
  94.9 5.3 fusion.5
  101.8 6.6 %stack.5 = bf16[32,384,2,256]{1,3,2,0:T(8,128)(2,1)} broadcast(bf16[384,2,256]{0,2,1:T(8,128)(2,1)S(1)} %pad_maximum_fusion), dimensions={1,2,3} | broadcast | bytes 12976128 | tf_op jit(solution)/shard_map/stack | solution.py:152
  108.4 6.3 %all-to-all-start = ((bf16[32,384,2,256]{1,3,2,0:T(8,128)(2,1)}), bf16[32,384,2,256]{1,3,2,0:T(8,128)(2,1)}, u32[]{:S(2)}, u32[]{:S(2)}) async-start(bf16[32,384,2,256]{1,3,2,0:T(8,128)(2,1)} %stack.5), calls=%async_computation | async-start | bytes 25165824 | tf_op jit(solution)/shard_map/all_to_all | solution.py:152
  116.2 92.3 %all-gather.8.cloned.1.call-done = bf16[256,3072]{1,0:T(8,128)(2,1)} async-done(((bf16[32,3072]{1,0:T(8,128)(2,1)}), bf16[256,3072]{1,0:T(8,128)(2,1)}) %all-gather.8.cloned.1.call-update) | async-done | bytes 1572880 | tf_op jit(solution)/shard_map/all_gather | solution.py:182
  208.5 4.8 fusion.7
  214.1 1.8 fusion.153
  215.8 1.4 fusion.154
  219.9 23.1 %all-gather = bf16[2080,128]{1,0:T(8,128)(2,1)S(1)} all-gather(bf16[520,128]{1,0:T(8,128)(2,1)S(1)} %pad_maximum_fusion.1), channel_id=2, replica_groups=mesh['blk_0'=4,'blk_1'=4,'blk_2'=2,'uly_0'=4,'uly_1'=2] {'blk_0'}, dimensions={0}, use_global_device_ids=true | all-gather | bytes 665600 | tf_op jit(solution)/shard_map/all_gather | solution.py:22
  244.9 161.0 %all-to-all-done = bf16[32,384,2,256]{1,3,2,0:T(8,128)(2,1)} async-done(((bf16[32,384,2,256]{1,3,2,0:T(8,128)(2,1)}), bf16[32,384,2,256]{1,3,2,0:T(8,128)(2,1)}, u32[]{:S(2)}, u32[]{:S(2)}) %all-to-all-start) | async-done | bytes 12582944 | tf_op jit(solution)/shard_map/all_to_all | solution.py:152
  406.0 16.6 %copy.73 = bf16[32,384,2,256]{3,1,0,2:T(8,128)(2,1)} copy(bf16[32,384,2,256]{1,3,2,0:T(8,128)(2,1)} %all-to-all-done) | data formatting | bytes 25165824 | tf_op jit(solution)/shard_map/all_to_all | solution.py:152
  422.6 110.9 %while.17 = (s32[]{:T(128)}, f32[2,384]{1,0:T(2,128)S(1)}, f32[2,384]{1,0:T(2,128)S(1)}, f32[2,384,128]{2,1,0:T(8,128)S(1)}, bf16[12288,2,256]{2,0,1:T(8,128)(2,...) while((s32[]{:T(128)}, f32[2,384]{1,0:T(2,128)S(1)}, ...), condition=%wide.region_12.13_spmd, body=%wide.region_9.12_spmd.sunk | while | flops 152962560 | bytes 6537391 | solution.py:161
  423.8 1.3 fusion.175
  427.3 1.3 fusion.175
  430.7 1.3 fusion.175
  434.2 1.3 fusion.175
  441.1 1.3 fusion.175
  444.6 1.3 fusion.175
  448.1 1.3 fusion.175
  451.5 1.3 fusion.175
  455.0 1.3 fusion.175
  458.5 1.3 fusion.175
  461.9 1.3 fusion.175
  465.4 1.3 fusion.175
  468.9 1.3 fusion.175
  475.8 1.3 fusion.175
  479.3 1.3 fusion.175
  482.7 1.3 fusion.175
  486.2 1.3 fusion.175
  489.7 1.3 fusion.175
  493.1 1.3 fusion.175
  496.6 1.3 fusion.175
  510.5 1.3 fusion.175
  513.9 1.3 fusion.175
  517.4 1.3 fusion.175
  520.9 1.3 fusion.175
  524.3 1.3 fusion.175
  527.8 1.3 fusion.175
  531.3 1.3 fusion.175
  533.7 2.2 convolution_convert_fusion
  536.9 17.1 %all-gather.1 = bf16[2080,128]{1,0:T(8,128)(2,1)S(1)} all-gather(bf16[520,128]{1,0:T(8,128)(2,1)S(1)} %copy-done.5), channel_id=3, replica_groups=mesh['blk_0'=4,'blk_1'=4,'blk_2'=2,'uly_0'=4,'uly_1'=2] {'blk_1'}, dimensions={0}, use_global_device_ids=true | all-gather | bytes 665600 | tf_op jit(solution)/shard_map/all_gather | solution.py:22
  554.5 2.0 all-gather.2
  558.3 1.8 convolution_convert_fusion.1
  560.0 5.0 all-to-all-start.1
  565.1 6.0 reduce-scatter.3.cloned.1.call-done
  571.2 48.0 %all-to-all-done.1 = bf16[8,32,3072]{2,1,0:T(8,128)(2,1)S(1)} async-done(((bf16[8,32,3072]{2,1,0:T(8,128)(2,1)}), bf16[8,32,3072]{2,1,0:T(8,128)(2,1)S(1)}, u32[]{:S(2)}, u32[]{:S(2)}) %all-to-all-start.1) | async-done | bytes 1572896 | tf_op jit(solution)/shard_map/all_to_all | solution.py:65
  620.1 1.7 multiply_convert_fusion
  (370 shorter events, 90.1 us)
Async XLA Ops:
  7.2 526.6 %copy-start = (bf16[256,3072]{1,0:T(8,128)(2,1)S(1)}, bf16[256,3072]{1,0:T(8,128)(2,1)}, u32[]{:S(2)}) copy-start(bf16[256,3072]{1,0:T(8,128)(2,1)} %param.18) | copy-start | bytes 4718596
  7.2 5.9 copy-start.13
  7.2 5.9 copy-start.12
  7.2 87.7 %all-gather.6.cloned.1.call-start = ((), (), s32[]{:S(2)}) async-start(), calls=%async_computation.4 | async-start | bytes 2654208 | tf_op jit(solution)/shard_map/all_gather | solution.py:177
  100.2 1.0 copy-start.1
  108.4 6.4 %copy-start.8 = (bf16[3,3072]{1,0:T(4,128)(2,1)S(1)}, bf16[3,3072]{1,0:T(4,128)(2,1)}, u32[]{:S(2)}) copy-start(bf16[3,3072]{1,0:T(4,128)(2,1)} %param.15) | copy-start | bytes 55300
  108.4 6.4 %copy-start.3 = (bf16[32,3072]{1,0:T(8,128)(2,1)S(1)}, bf16[32,3072]{1,0:T(8,128)(2,1)}, u32[]{:S(2)}) copy-start(bf16[32,3072]{1,0:T(8,128)(2,1)} %param.13) | copy-start | bytes 589828
  108.4 297.5 %all-to-all-start = ((bf16[32,384,2,256]{1,3,2,0:T(8,128)(2,1)}), bf16[32,384,2,256]{1,3,2,0:T(8,128)(2,1)}, u32[]{:S(2)}, u32[]{:S(2)}) async-start(bf16[32,384,2,256]{1,3,2,0:T(8,128)(2,1)} %stack.5), calls=%async_computation | async-start | bytes 25165824 | tf_op jit(solution)/shard_map/all_to_all | solution.py:152
  114.8 93.7 %all-gather.8.cloned.1.call-start = ((), (), s32[]{:S(2)}) async-start(), calls=%async_computation.5 | async-start | bytes 1769472 | tf_op jit(solution)/shard_map/all_gather | solution.py:182
  116.1 455.0 %reduce-scatter.3.cloned.1.call-start = ((), (), s32[]{:S(2)}) async-start(), calls=%async_computation.6 | async-start | bytes 2949120 | tf_op jit(solution)/shard_map/reduce_scatter | solution.py:54
  213.7 30.9 %copy-start.6 = (bf16[256,1,2,128]{3,0,2,1:T(8,128)(2,1)}, bf16[256,1,2,128]{3,0,2,1:T(8,128)(2,1)S(1)}, u32[]{:S(2)}) copy-start(bf16[256,1,2,128]{3,0,2,1:T(8,128)(2,1)S(1)} %copy.98) | copy-start | bytes 393220
  536.0 0.9 copy-start.5
  536.9 20.0 %copy-start.11 = (f32[2,256]{1,0:T(2,128)S(1)}, f32[2,256]{1,0:T(2,128)}, u32[]{:S(2)}) copy-start(f32[2,256]{1,0:T(2,128)} %get-tuple-element.188) | copy-start | bytes 6148
  536.9 20.0 %copy-start.2 = (f32[2,256,256]{1,2,0:T(8,128)S(1)}, f32[2,256,256]{1,2,0:T(8,128)}, u32[]{:S(2)}) copy-start(f32[2,256,256]{1,2,0:T(8,128)} %get-tuple-element.189) | copy-start | bytes 1572868
  554.0 3.0 copy-start.7
  556.9 1.4 copy-start.4
  560.0 5.0 copy-start.9
  560.0 11.1 %copy-start.10 = (bf16[3,3072]{1,0:T(4,128)(2,1)S(1)}, bf16[3,3072]{1,0:T(4,128)(2,1)}, u32[]{:S(2)}) copy-start(bf16[3,3072]{1,0:T(4,128)(2,1)} %param.14) | copy-start | bytes 55300
  560.0 59.1 %all-to-all-start.1 = ((bf16[8,32,3072]{2,1,0:T(8,128)(2,1)}), bf16[8,32,3072]{2,1,0:T(8,128)(2,1)S(1)}, u32[]{:S(2)}, u32[]{:S(2)}) async-start(bf16[8,32,3072]{2,1,0:T(8,128)(2,1)} %bitcast.69), calls=%async_computation.3 | async-start | bytes 3145728 | tf_op jit(solution)/shard_map/all_to_all | solution.py:65
  565.0 55.1 %reduce-scatter.5.cloned.1.call-start = ((), (), s32[]{:S(2)}) async-start(), calls=%async_computation.7 | async-start | bytes 884736 | tf_op jit(solution)/shard_map/reduce_scatter | solution.py:54
Sparse Core Ops, SparseCore 0:
  13.2 81.6 all-gather.5
  118.7 89.7 all-gather.7
  536.1 34.9 reduce-scatter.2
  573.5 44.1 reduce-scatter.4
